TPU v7x, 512 devices: a whole 4x4x16 slice. The times are simulated.
512 devices in a mesh: rows: 64 (over z, y), cols: 8 (over x, core).
Axes of the slice: x: 4, y: 4, z: 16, core: 2. Of those that a mesh axis runs over, the one named last changes fastest.
Arguments:
- x_start: float32 [96, 32768], P('cols', 'rows'), may hold values from -6 to 6
- p_start: float32 [96, 32768], P('cols', 'rows'), may hold values from -6 to 6
- k_diag: bfloat16 [512, 64, 64], P('rows'), as said below
- k_link: bfloat16 [512, 4, 64, 64], P('rows')
- m_diag: bfloat16 [512, 64, 64], P('rows'), as said below
- m_link: bfloat16 [512, 4, 64, 64], P('rows')
- link_to: int32 [512, 4], P('rows'), may hold values from 0 to 7, as said below
- link_count: int32 [512], P('rows'), may hold values from 1 to 4, as said below
- k_iface: bfloat16 [64, 64, 3, 64, 64], P('rows'), as said below
- m_iface: bfloat16 [64, 64, 3, 64, 64], P('rows'), as said below
- iface_local: int32 [64, 64, 3], P('rows'), may hold values from 0 to 7, as said below
- iface_live: int32 [64, 64, 3], P('rows'), may hold values from 0 to 1, as said below
Outputs:
- x_out: float32 [96, 32768], P('cols', 'rows')
- p_out: float32 [96, 32768], P('cols', 'rows')
- ritz: float32 [96, 96], replicated
Inputs may be any that keep to these rules, and one draw needn't show every extreme that they name: `link_to`: for each row owner and each b < 4, the b-th links of its 8 supernodes form a permutation of its supernodes. `link_count`: the first supernode of every row owner has all 4 links live. `iface_local`: each row owner's 192 slots name each of its supernodes at most (199) // 8 times. iface_live[p, q, c] = iface_live[q, p, c], and it is 0 where p = q. `k_iface`: for p < q the block for (q, p, c) is the transpose of the block for (p, q, c). `m_iface`: for p < q the block for (q, p, c) is the transpose of the block for (p, q, c). `k_diag`: every block is symmetric with diagonal entries of 1 or more. `m_diag`: every block is symmetric with diagonal entries of 1 or more.
All inputs are finite; a program needn't handle non-finite values.
Results may differ from a plain program's by a relative error of at most 0.0003.
Values sent between devices are 32-bit elements; how exact they have to be, the bound alone decides.
No kernel may reach another device: no remote copies, remote signals or barrier semaphores. Data moves between devices by JAX's collectives and lax.ppermute only.
A program may use at most 128 MiB of HBM per device.

v0:
```python
import jax
import jax.numpy as jnp
from jax import lax
from jax.sharding import PartitionSpec as P

STEPS = 2
RR_ITERS = 3
exact_dots = lax.Precision.HIGHEST


def symmetric(matrix):
    return 0.5 * (matrix + matrix.T)


def local_product(vectors, diag_blocks, link_blocks, link_onehot, link_live):
    near = (
        jnp.einsum("sbt,ctj->csbj", link_onehot, vectors, precision=exact_dots)
        * link_live[None, :, :, None]
    )
    result = jnp.einsum(
        "sij,csj->csi", diag_blocks.astype(jnp.float32), vectors, precision=exact_dots
    )
    result = result + jnp.einsum(
        "sbij,csbj->csi", link_blocks.astype(jnp.float32), near, precision=exact_dots
    )
    back = (
        jnp.einsum("sbji,csj->csbi", link_blocks.astype(jnp.float32), vectors, precision=exact_dots)
        * link_live[None, :, :, None]
    )
    return result + jnp.einsum("sbt,csbi->cti", link_onehot, back, precision=exact_dots)


def apply_pair(vectors, tables):
    (
        k_diag,
        k_link,
        m_diag,
        m_link,
        link_onehot,
        link_live,
        k_faces,
        m_faces,
        slot_onehot,
        slot_live,
    ) = tables
    col_count, row_count = vectors.shape
    node_count = link_onehot.shape[0]
    node_size = k_diag.shape[1]
    split_vec = vectors.reshape(col_count, node_count, node_size)
    picked = jnp.einsum("ks,csj->kcj", slot_onehot, split_vec, precision=exact_dots)
    owners = lax.axis_size("rows")

    def face_term(faces):
        term = (
            jnp.einsum("kij,kcj->kci", faces.astype(jnp.float32), picked, precision=exact_dots)
            * slot_live[:, None, None]
        )
        return term.reshape(owners, -1)

    recv_k, recv_m = (
        lax.all_to_all(face_term(k_faces), "rows", split_axis=0, concat_axis=0, tiled=True),
        lax.all_to_all(face_term(m_faces), "rows", split_axis=0, concat_axis=0, tiled=True),
    )

    def finish(diag_blocks, link_blocks, received):
        local = local_product(split_vec, diag_blocks, link_blocks, link_onehot, link_live)
        arrived = jnp.einsum(
            "ks,kci->csi",
            slot_onehot,
            received.reshape(-1, col_count, node_size),
            precision=exact_dots,
        )
        return (local + arrived).reshape(col_count, row_count)

    return (finish(k_diag, k_link, recv_k), finish(m_diag, m_link, recv_m))


def gram_pair(own_s, own_k, own_m):
    blocks, col_part, row_count = own_s.shape
    modes = col_part * lax.axis_size("cols")
    dof_count = row_count * lax.axis_size("rows")
    empty = jnp.zeros((blocks, modes, blocks, col_part), jnp.float32)
    panel_rows = lax.all_gather(own_s, "cols", axis=1, tiled=True)
    offset = jnp.int32(0)
    term_k = jnp.einsum("anr,bcr->anbc", panel_rows, own_k, precision=exact_dots)
    term_m = jnp.einsum("anr,bcr->anbc", panel_rows, own_m, precision=exact_dots)
    part_k = lax.dynamic_update_slice_in_dim(empty, term_k, offset, 1)
    part_m = lax.dynamic_update_slice_in_dim(empty, term_m, offset, 1)
    summed_k, summed_m = lax.psum((part_k, part_m), "rows")
    full_k, full_m = (
        lax.all_gather(summed_k, "cols", axis=3, tiled=True),
        lax.all_gather(summed_m, "cols", axis=3, tiled=True),
    )
    extent = blocks * modes
    return (
        symmetric(full_k.reshape(extent, extent) / dof_count),
        symmetric(full_m.reshape(extent, extent) / dof_count),
        own_s,
    )


def rayleigh(gram_stiff, gram_mass, modes):
    total = gram_stiff.shape[0]
    factor = jnp.linalg.cholesky(gram_stiff)
    coeffs = jnp.eye(total, modes, dtype=jnp.float32)
    for inner_index in range(RR_ITERS):
        solved = jax.scipy.linalg.cho_solve(
            (factor, True), jnp.dot(gram_mass, coeffs, precision=exact_dots)
        )
        inner = symmetric(
            jnp.dot(
                solved.T, jnp.dot(gram_mass, solved, precision=exact_dots), precision=exact_dots
            )
        )
        inner_factor = jnp.linalg.cholesky(inner)
        coeffs = jax.scipy.linalg.solve_triangular(inner_factor, solved.T, lower=True).T
    ritz_new = symmetric(
        jnp.dot(coeffs.T, jnp.dot(gram_stiff, coeffs, precision=exact_dots), precision=exact_dots)
    )
    return (coeffs, ritz_new)


def contract(coef, panel_rows):
    new_x = jnp.einsum("anc,anr->cr", coef, panel_rows, precision=exact_dots)
    new_p = jnp.einsum("anc,anr->cr", coef[1:], panel_rows[1:], precision=exact_dots)
    return (new_x, new_p)


def own_columns(coeffs, blocks, col_part):
    modes = coeffs.shape[1]
    col_start = lax.axis_index("cols") * col_part
    return lax.dynamic_slice_in_dim(coeffs.reshape(blocks, modes, modes), col_start, col_part, 2)


def mass_mixture(mass_x, ritz_now):
    col_part, row_count = mass_x.shape
    col_start = lax.axis_index("cols") * col_part
    coef = lax.dynamic_slice_in_dim(ritz_now, col_start, col_part, 1)
    panel_rows = lax.all_gather(mass_x, "cols", axis=0, tiled=True)
    part = lax.slice_in_dim(coef, 0, panel_rows.shape[0], axis=0)
    return jnp.zeros((col_part, row_count), jnp.float32) + jnp.einsum(
        "nc,nr->cr", part, panel_rows, precision=exact_dots
    )


def body(
    x_start,
    p_start,
    k_diag,
    k_link,
    m_diag,
    m_link,
    link_to,
    link_count,
    k_iface,
    m_iface,
    iface_local,
    iface_live,
):
    col_part, row_count = x_start.shape
    modes = col_part * lax.axis_size("cols")
    node_count, link_slots = link_to.shape
    node_size = k_diag.shape[1]
    node_ids = jnp.arange(node_count, dtype=jnp.int32)
    link_onehot = (link_to[:, :, None] == node_ids[None, None, :]).astype(jnp.float32)
    link_live = (jnp.arange(link_slots, dtype=jnp.int32)[None, :] < link_count[:, None]).astype(
        jnp.float32
    )
    local_slots = iface_local.reshape(-1)
    slot_onehot = (local_slots[:, None] == node_ids[None, :]).astype(jnp.float32)
    slot_live = iface_live.reshape(-1).astype(jnp.float32)
    k_faces = k_iface.reshape(-1, node_size, node_size)
    m_faces = m_iface.reshape(-1, node_size, node_size)
    tables = (
        k_diag,
        k_link,
        m_diag,
        m_link,
        link_onehot,
        link_live,
        k_faces,
        m_faces,
        slot_onehot,
        slot_live,
    )
    precond = 1.0 / jnp.diagonal(k_diag.astype(jnp.float32), axis1=1, axis2=2).reshape(-1)
    both_k, both_m = apply_pair(jnp.concatenate([x_start, p_start], 0), tables)
    stiff_x, stiff_p = (both_k[:col_part], both_k[col_part:])
    mass_x, mass_p = (both_m[:col_part], both_m[col_part:])
    x_block, p_block = (x_start, p_start)
    stiff_gram, mass_gram, unused = gram_pair(x_block[None], stiff_x[None], mass_x[None])
    ritz_now = jax.scipy.linalg.cho_solve((jnp.linalg.cholesky(mass_gram), True), stiff_gram)
    for step_index in range(STEPS):
        resid = stiff_x - mass_mixture(mass_x, ritz_now)
        search = resid * precond[None, :]
        stiff_w, mass_w = apply_pair(search, tables)
        own_s = jnp.stack([x_block, search, p_block], 0)
        own_k = jnp.stack([stiff_x, stiff_w, stiff_p], 0)
        own_m = jnp.stack([mass_x, mass_w, mass_p], 0)
        gram_stiff, gram_mass, whole = gram_pair(own_s, own_k, own_m)
        coeffs, ritz_new = rayleigh(gram_stiff, gram_mass, modes)
        mine = own_columns(coeffs, 3, col_part)
        empty = jnp.zeros((col_part, row_count), jnp.float32)
        panel_rows = lax.all_gather(own_s, "cols", axis=1, tiled=True)
        add_coef = lax.slice_in_dim(mine, 0, panel_rows.shape[1], axis=1)
        new_x, new_p = contract(add_coef, panel_rows)
        x_block = empty + new_x
        p_block = empty + new_p
        if step_index + 1 < STEPS:
            blank = jnp.zeros((col_part, row_count), jnp.float32)
            panels = (
                lax.all_gather(own_k, "cols", axis=1, tiled=True),
                lax.all_gather(own_m, "cols", axis=1, tiled=True),
            )
            coef = lax.slice_in_dim(mine, 0, panels[0].shape[1], axis=1)
            new_kx, new_kp = contract(coef, panels[0])
            new_mx, new_mp = contract(coef, panels[1])
            stiff_x = blank + new_kx
            stiff_p = blank + new_kp
            mass_x = blank + new_mx
            mass_p = blank + new_mp
        ritz_now = ritz_new
    return (x_block, p_block, ritz_now)


def solution(mesh):
    placed = (
        P("cols", "rows"),
        P("cols", "rows"),
        P("rows", None, None),
        P("rows", None, None, None),
        P("rows", None, None),
        P("rows", None, None, None),
        P("rows", None),
        P("rows"),
        P("rows", None, None, None, None),
        P("rows", None, None, None, None),
        P("rows", None, None),
        P("rows", None, None),
    )
    return jax.shard_map(
        body,
        mesh=mesh,
        in_specs=placed,
        out_specs=(P("cols", "rows"), P("cols", "rows"), P()),
        check_vma=False,
    )
```

profile of v0, /device:TPU:1, one launch (start us, length us, event | category | flops | bytes accessed | tf_op | source)
XLA Modules:
  0.0 1823.3 jit_solution(2422586496049059222)
XLA Ops:
  14.4 9.0 convolution_multiply_fusion
  23.4 3.7 all_to_all.49
  27.0 19.5 %all-to-all-start.1 = ((f32[64,1,4608]{2,1,0:T(1,128)}), f32[64,1,4608]{2,1,0:T(1,128)}, u32[]{:S(2)}, u32[]{:S(2)}) async-start(f32[64,1,4608]{2,1,0:T(1,128)} %all_to_all.49), calls=%async_computation.1 | async-start | bytes 2359296 | tf_op jit(solution)/shard_map/all_to_all | solution.py:62
  46.6 7.4 convolution_multiply_fusion.1
  54.0 3.7 all_to_all.48
  57.7 45.7 %all-to-all-done.1 = f32[64,1,4608]{2,1,0:T(1,128)} async-done(((f32[64,1,4608]{2,1,0:T(1,128)}), f32[64,1,4608]{2,1,0:T(1,128)}, u32[]{:S(2)}, u32[]{:S(2)}) %all-to-all-start.1) | async-done | bytes 1179680 | tf_op jit(solution)/shard_map/all_to_all | solution.py:62
  103.3 9.9 all-to-all-start
  114.1 15.6 all-gather.1
  141.7 5.1 reduce.17
  157.5 11.7 all-to-all-done
  169.2 5.1 reduce.16
  183.8 222.6 %all-reduce.5 = (f32[1,96,1,12]{1,3,2,0:T(8,128)S(1)}, f32[1,96,1,12]{1,3,2,0:T(8,128)S(1)}) all-reduce(f32[1,96,1,12]{1,3,2,0:T(8,128)S(1)} %convolution_bitcast_fusion.19, f32[1,96,1,12]{1,3,2,0:T(8,128)S(1)} %convolution_bitcast_fusion.20), channel_id=1, replica_groups=mesh['rows'=64,'cols'=8] {'rows'}, use_global_device_ids=true, to_apply=%region_3.5 | all-reduce | flops 2304 | bytes 18432 | tf_op jit(solution)/shard_map/psum | solution.py:89
  406.3 71.9 %all_gather.42 = f32[1,96,1,96]{1,2,0,3:T(1,128)S(1)} all-gather(f32[1,96,1,12]{1,2,0,3:T(1,128)S(1)} %copy.371), channel_id=1, replica_groups=mesh['rows'=64,'cols'=8] {'cols'}, dimensions={3}, use_global_device_ids=true | all-gather | bytes 41472 | tf_op jit(solution)/shard_map/all_gather | solution.py:92
  478.6 8.8 cholesky.329
  488.7 7.4 custom-call.31
  496.1 12.8 all_gather.43
  510.2 12.8 all-gather.2
  529.5 7.6 convolution_multiply_fusion.5
  540.0 6.5 all-to-all-start.2
  548.3 8.5 convolution_multiply_fusion.4
  562.8 17.3 all-to-all-done.2
  580.1 7.5 all-to-all-start.3
  599.7 16.2 all_gather.45
  615.9 3.3 reduce.18
  629.2 3.3 reduce.19
  642.4 14.5 all_gather.48
  656.9 13.4 all_gather.49
  673.4 234.2 %all-reduce.11.cloned.1.call-done = (f32[3,96,3,12]{1,3,2,0:T(8,128)}, f32[3,96,3,12]{1,3,2,0:T(8,128)}) async-done(((f32[3,96,3,12]{1,3,2,0:T(8,128)}, f32[3,96,3,12]{1,3,2,0:T(8,128)}), (f32[3,96,3,12]{1,3,2,0:T(8,128)}, f32[3,96,3,12]{1,3,2,0:T(8,128)})) %all-reduce.11.cloned.1.call-update) | async-done | bytes 82960 | tf_op jit(solution)/shard_map/psum | solution.py:89
  908.5 25.0 %all_gather.46 = f32[3,96,3,96]{1,2,0,3:T(4,128)} all-gather(f32[3,96,3,12]{1,2,0,3:T(4,128)S(1)} %copy.399), channel_id=1, replica_groups=mesh['rows'=64,'cols'=8] {'cols'}, dimensions={3}, use_global_device_ids=true | all-gather | bytes 373248 | tf_op jit(solution)/shard_map/all_gather | solution.py:91
  947.7 11.7 cholesky.342
  960.3 9.8 custom-call.46
  973.0 11.7 cholesky.361
  985.4 10.2 custom-call.47
  1006.0 5.8 while.12
  1012.4 29.5 %custom-call.52 = f32[3,128,128]{1,2,0:T(8,128)S(1)} custom-call(f32[3,128,128]{2,1,0:T(8,128)S(1)} %pad_maximum_fusion), custom_call_target="InvertDiagBlocksLowerTriangular" | custom-call | tf_op jit(solution)/shard_map/jit(_cho_solve)/triangular_solve | solution.py:107
  1042.8 14.3 all_gather.47
  1079.9 9.6 cholesky.397
  1091.4 8.2 custom-call.49
  1113.7 9.7 cholesky.408
  1125.3 8.2 custom-call.51
  1143.6 8.8 cholesky.419
  1153.7 7.4 custom-call.53
  1170.4 13.0 all-gather.3
  1190.5 7.5 convolution_multiply_fusion.3
  1201.1 9.1 all-to-all-start.4
  1212.3 8.5 convolution_multiply_fusion.2
  1228.7 15.0 all-to-all-done.4
  1243.7 7.5 all-to-all-start.5
  1262.0 15.7 all_gather.51
  1304.6 248.9 %all-reduce.9.cloned.1.call-done = (f32[3,96,3,12]{1,3,2,0:T(8,128)}, f32[3,96,3,12]{1,3,2,0:T(8,128)}) async-done(((f32[3,96,3,12]{1,3,2,0:T(8,128)}, f32[3,96,3,12]{1,3,2,0:T(8,128)}), (f32[3,96,3,12]{1,3,2,0:T(8,128)}, f32[3,96,3,12]{1,3,2,0:T(8,128)})) %all-reduce.9.cloned.1.call-update) | async-done | bytes 82960 | tf_op jit(solution)/shard_map/psum | solution.py:89
  1554.4 25.0 %all_gather.52 = f32[3,96,3,96]{1,2,0,3:T(4,128)} all-gather(f32[3,96,3,12]{1,2,0,3:T(4,128)S(1)} %copy.458), channel_id=1, replica_groups=mesh['rows'=64,'cols'=8] {'cols'}, dimensions={3}, use_global_device_ids=true | all-gather | bytes 373248 | tf_op jit(solution)/shard_map/all_gather | solution.py:91
  1593.6 11.7 cholesky.432
  1606.1 9.8 custom-call.54
  1618.9 11.7 cholesky.451
  1632.5 10.1 custom-call.55
  1652.4 5.8 while.13
  1658.3 29.5 %custom-call.60 = f32[3,128,128]{1,2,0:T(8,128)S(1)} custom-call(f32[3,128,128]{2,1,0:T(8,128)S(1)} %pad_maximum_fusion.1), custom_call_target="InvertDiagBlocksLowerTriangular" | custom-call | tf_op jit(solution)/shard_map/jit(_cho_solve)/triangular_solve | solution.py:107
  1688.7 14.3 all_gather.53
  1725.8 9.6 cholesky.487
  1737.4 8.2 custom-call.57
  1759.6 9.7 cholesky.498
  1771.3 8.2 custom-call.59
  1789.5 8.8 cholesky.509
  1799.6 7.4 custom-call.61
  (501 shorter events, 345.6 us)
Async XLA Ops:
  7.2 39.4 %copy-start = (bf16[1,64,3,64,64]{4,3,2,1,0:T(8,128)(2,1)S(1)}, bf16[1,64,3,64,64]{4,3,2,1,0:T(8,128)(2,1)}, u32[]{:S(2)}) copy-start(bf16[1,64,3,64,64]{4,3,2,1,0:T(8,128)(2,1)} %param.26) | copy-start | bytes 4718596
  8.2 516.8 %copy-start.48 = (s32[192]{0:T(256)}, s32[192]{0:T(256)S(1)}, u32[]{:S(2)}) copy-start(s32[192]{0:T(256)S(1)} %eq.37) | copy-start | bytes 2308
  11.1 3.0 copy-start.57
  14.4 32.2 %copy-start.54 = (f32[192]{0:T(256)}, f32[192]{0:T(256)S(1)}, u32[]{:S(2)}) copy-start(f32[192]{0:T(256)S(1)} %convert_element_type.19) | copy-start | bytes 2308
  27.0 76.3 %all-to-all-start.1 = ((f32[64,1,4608]{2,1,0:T(1,128)}), f32[64,1,4608]{2,1,0:T(1,128)}, u32[]{:S(2)}, u32[]{:S(2)}) async-start(f32[64,1,4608]{2,1,0:T(1,128)} %all_to_all.49), calls=%async_computation.1 | async-start | bytes 2359296 | tf_op jit(solution)/shard_map/all_to_all | solution.py:62
  57.7 56.3 %copy-start.58 = (s32[8]{0:T(128)S(1)}, s32[8]{0:T(128)}, u32[]{:S(2)}) copy-start(s32[8]{0:T(128)} %param.25) | copy-start | bytes 100
  57.7 56.4 %copy-start.31 = (f32[12,512]{1,0:T(8,128)S(1)}, f32[12,512]{1,0:T(8,128)}, u32[]{:S(2)}) copy-start(f32[12,512]{1,0:T(8,128)} %param.18) | copy-start | bytes 73732
  57.7 73.7 %copy-start.11 = (bf16[8,64,64]{2,1,0:T(8,128)(2,1)S(1)}, bf16[8,64,64]{2,1,0:T(8,128)(2,1)}, u32[]{:S(2)}) copy-start(bf16[8,64,64]{2,1,0:T(8,128)(2,1)} %param.20) | copy-start | bytes 196612
  103.3 65.9 %all-to-all-start = ((f32[64,1,4608]{2,1,0:T(1,128)}), f32[64,1,4608]{2,1,0:T(1,128)}, u32[]{:S(2)}, u32[]{:S(2)}) async-start(f32[64,1,4608]{2,1,0:T(1,128)} %all_to_all.48), calls=%async_computation | async-start | bytes 2359296 | tf_op jit(solution)/shard_map/all_to_all | solution.py:61
  114.0 481.8 %copy-start.52 = (f32[8,4]{0,1:T(4,128)}, f32[8,4]{0,1:T(4,128)S(1)}, u32[]{:S(2)}) copy-start(f32[8,4]{0,1:T(4,128)S(1)} %fusion.359) | copy-start | bytes 388
  114.1 479.4 %copy-start.43 = (f32[8,4]{1,0:T(8,128)}, f32[8,4]{1,0:T(8,128)S(1)}, u32[]{:S(2)}) copy-start(f32[8,4]{1,0:T(8,128)S(1)} %copy.351) | copy-start | bytes 388
  131.4 5.4 copy-start.45
  135.4 2.6 copy-start.4
  135.4 5.0 copy-start.13
  136.9 4.5 copy-start.30
  149.8 2.8 copy-start.5
  149.8 2.8 copy-start.27
  149.8 2.8 copy-start.29
  177.2 2.8 copy-start.3
  177.2 2.8 copy-start.25
  177.2 2.8 copy-start.28
  180.7 329.6 %copy-start.33 = (f32[1,12,512]{2,1,0:T(8,128)S(1)}, f32[1,12,512]{2,1,0:T(8,128)}, u32[]{:S(2)}) copy-start(f32[1,12,512]{2,1,0:T(8,128)} %reshape.261) | copy-start | bytes 73732
  525.0 4.4 copy-start.55
  540.0 40.0 %all-to-all-start.2 = ((f32[64,1,2304]{2,1,0:T(1,128)}), f32[64,1,2304]{2,1,0:T(1,128)}, u32[]{:S(2)}, u32[]{:S(2)}) async-start(f32[64,1,2304]{2,1,0:T(1,128)} %all_to_all.50), calls=%async_computation.2 | async-start | bytes 1179648 | tf_op jit(solution)/shard_map/all_to_all | solution.py:61
  556.8 3.6 copy-start.32
  556.8 3.6 copy-start.47
  562.8 34.2 %copy-start.12 = (bf16[8,64,64]{2,1,0:T(8,128)(2,1)S(1)}, bf16[8,64,64]{2,1,0:T(8,128)(2,1)}, u32[]{:S(2)}) copy-start(bf16[8,64,64]{2,1,0:T(8,128)(2,1)} %param.20) | copy-start | bytes 196612
  580.1 49.1 %all-to-all-start.3 = ((f32[64,1,2304]{2,1,0:T(1,128)}), f32[64,1,2304]{2,1,0:T(1,128)}, u32[]{:S(2)}, u32[]{:S(2)}) async-start(f32[64,1,2304]{2,1,0:T(1,128)} %all_to_all.51), calls=%async_computation.3 | async-start | bytes 1179648 | tf_op jit(solution)/shard_map/all_to_all | solution.py:62
  587.6 320.0 %all-reduce.11.cloned.1.call-start = ((), (), s32[]{:S(2)}) async-start(), calls=%async_computation.7 | async-start | bytes 294912 | tf_op jit(solution)/shard_map/psum | solution.py:89
  593.5 6.2 copy-start.26
  619.2 4.8 copy-start.38
  619.2 4.8 copy-start.41
  621.8 3.9 copy-start.20
  629.2 5.9 copy-start.49
  635.0 4.0 copy-start.19
  947.0 0.8 copy-start.15
  947.7 57.5 %copy-start.61 = (s32[2]{0:T(128)S(1)}, s32[2]{0:T(128)}, u32[]{:S(2)}) copy-start(s32[2]{0:T(128)} %iota_multiply_fusion) | copy-start | bytes 28
  960.3 51.5 %copy-start.17 = (f32[128,96]{1,0:T(8,128)S(1)}, f32[128,96]{1,0:T(8,128)}, u32[]{:S(2)}) copy-start(f32[128,96]{1,0:T(8,128)} %pad_convert_fusion) | copy-start | bytes 147460
  1005.2 0.8 copy-start.7
  1066.5 0.8 copy-start.1
  1141.0 12.7 copy-start.16
  1169.8 0.6 copy-start.35
  1185.4 5.1 copy-start.56
  1201.1 42.7 %all-to-all-start.4 = ((f32[64,1,2304]{2,1,0:T(1,128)}), f32[64,1,2304]{2,1,0:T(1,128)}, u32[]{:S(2)}, u32[]{:S(2)}) async-start(f32[64,1,2304]{2,1,0:T(1,128)} %all_to_all.52), calls=%async_computation.4 | async-start | bytes 1179648 | tf_op jit(solution)/shard_map/all_to_all | solution.py:61
  1220.8 3.0 copy-start.44
  1220.8 4.4 copy-start.46
  1223.8 3.7 copy-start.10
  1228.7 26.5 %copy-start.53 = (f32[8,4]{0,1:T(4,128)S(1)}, f32[8,4]{0,1:T(4,128)}, u32[]{:S(2)}) copy-start(f32[8,4]{0,1:T(4,128)} %copy-done.52) | copy-start | bytes 388
  1243.7 43.8 %all-to-all-start.5 = ((f32[64,1,2304]{2,1,0:T(1,128)}), f32[64,1,2304]{2,1,0:T(1,128)}, u32[]{:S(2)}, u32[]{:S(2)}) async-start(f32[64,1,2304]{2,1,0:T(1,128)} %all_to_all.53), calls=%async_computation.5 | async-start | bytes 1179648 | tf_op jit(solution)/shard_map/all_to_all | solution.py:62
  1251.3 302.2 %all-reduce.9.cloned.1.call-start = ((), (), s32[]{:S(2)}) async-start(), calls=%async_computation.6 | async-start | bytes 294912 | tf_op jit(solution)/shard_map/psum | solution.py:89
  1252.8 7.2 copy-start.8
  1252.8 8.2 copy-start.9
  1277.7 5.9 copy-start.50
  1281.0 4.8 copy-start.37
  1281.0 4.8 copy-start.40
  1287.5 5.9 copy-start.51
  1290.8 4.8 copy-start.39
  1293.4 3.9 copy-start.36
  1293.4 6.5 copy-start.34
  1592.8 0.8 copy-start.14
  1593.6 58.8 %copy-start.60 = (s32[2,2]{1,0:T(2,128)S(1)}, s32[2,2]{1,0:T(2,128)}, u32[]{:S(2)}) copy-start(s32[2,2]{1,0:T(2,128)} %copy-done.59) | copy-start | bytes 52
  1606.1 52.1 %copy-start.18 = (f32[128,96]{1,0:T(8,128)S(1)}, f32[128,96]{1,0:T(8,128)}, u32[]{:S(2)}) copy-start(f32[128,96]{1,0:T(8,128)} %pad_convert_fusion) | copy-start | bytes 147460
  1651.6 0.8 copy-start.6
  1712.5 0.8 copy-start.2
  (6 other events, 3.7 us)
Sparse Core Ops, SparseCore 0:
  657.0 250.5 all-reduce.10
  1302.6 250.8 all-reduce.8
where the time goes:
time: 1840 us; the launch traced here: 1820 us
  waiting for transfers between devices  573 us (31%)
  blocking collectives  487 us (26%)
  other arithmetic  339 us (18%)
  matrix products  201 us (11%)
  local copies, waits for them, and re-layouts  144 us (8%)
  starting transfers between devices  60.1 us (3%)
  between operations  19.9 us (1%)
    psum x2, waiting for transfers between devices, gram_pair(): summed_k, summed_m = lax.psum((part_k, part_m), 'rows')  483 us
    psum x1, blocking collectives, gram_pair(): summed_k, summed_m = lax.psum((part_k, part_m), 'rows')  223 us
    all_gather x3, blocking collectives, gram_pair(): lax.all_gather(summed_m, 'cols', axis=3, tiled=True)  100 us
    another operation x21, other arithmetic, rayleigh(): factor = jnp.linalg.cholesky(gram_stiff)  98.4 us
    all_gather x3, blocking collectives, gram_pair(): lax.all_gather(summed_k, 'cols', axis=3, tiled=True)  62.8 us
    another operation x11, other arithmetic, rayleigh(): jax.scipy.linalg.cho_solve((factor, True), jnp.dot(gram_mass, coeffs, pre...  62.4 us
    another operation x18, other arithmetic, rayleigh(): inner_factor = jnp.linalg.cholesky(inner)  60.2 us
    another operation x12, other arithmetic, rayleigh(): jax.scipy.linalg.solve_triangular(inner_factor, solved.T, lower=True)  53.7 us
  transfers between devices with their start and end apart: 8, of which 6 were waited for; matrix products, arithmetic and copies ran while one was open for 6% of the time, Pallas kernels for 0%

commit v1 on v0

--- a/solution.py
+++ b/solution.py
@@ -80,7 +80,15 @@
     modes = col_part * lax.axis_size("cols")
     dof_count = row_count * lax.axis_size("rows")
     empty = jnp.zeros((blocks, modes, blocks, col_part), jnp.float32)
-    panel_rows = lax.all_gather(own_s, "cols", axis=1, tiled=True)
+    panel_rows = jnp.concatenate(
+        jax.lax.all_to_all(
+            jnp.stack([own_s for _ in range(jax.lax.psum(1, axis_name="cols"))]),
+            "cols",
+            concat_axis=0,
+            split_axis=0,
+        ),
+        axis=1,
+    )
     offset = jnp.int32(0)
     term_k = jnp.einsum("anr,bcr->anbc", panel_rows, own_k, precision=exact_dots)
     term_m = jnp.einsum("anr,bcr->anbc", panel_rows, own_m, precision=exact_dots)

time: 1840 us -> 1850 us (level)
    psum x2, waiting for transfers between devices: 483 us -> 453 us  [gram_pair(): summed_k, summed_m = lax.psum((part_k, part_m), 'rows')]
    all_to_all x0 -> x3, starting transfers between devices: none -> 18.9 us  [gram_pair(): jax.lax.all_to_all(jnp.stack([own_s for _ in range(jax.lax.psum(1, axis_n...]
    all_gather x3 -> x2, blocking collectives: 47.5 us -> 33.1 us  [body(): panel_rows = lax.all_gather(own_s, 'cols', axis=1, tiled=True)]
  transfers between devices with their start and end apart: 8 -> 11, of which waited for: 6 -> 8; matrix products, arithmetic and copies ran while one was open for 6% -> 9% of each run, Pallas kernels for 0% -> 0%
where the time goes in v1:
time: 1850 us; the launch traced here: 1830 us
  waiting for transfers between devices  562 us (30%)
  blocking collectives  475 us (26%)
  other arithmetic  342 us (18%)
  matrix products  202 us (11%)
  local copies, waits for them, and re-layouts  151 us (8%)
  starting transfers between devices  77.9 us (4%)
  between operations  20.2 us (1%)
    psum x2, waiting for transfers between devices, gram_pair(): summed_k, summed_m = lax.psum((part_k, part_m), 'rows')  453 us
    psum x1, blocking collectives, gram_pair(): summed_k, summed_m = lax.psum((part_k, part_m), 'rows')  222 us
    all_gather x3, blocking collectives, gram_pair(): lax.all_gather(summed_m, 'cols', axis=3, tiled=True)  100 us
    another operation x21, other arithmetic, rayleigh(): factor = jnp.linalg.cholesky(gram_stiff)  97.9 us
    all_gather x3, blocking collectives, gram_pair(): lax.all_gather(summed_k, 'cols', axis=3, tiled=True)  63.4 us
    another operation x11, other arithmetic, rayleigh(): jax.scipy.linalg.cho_solve((factor, True), jnp.dot(gram_mass, coeffs, pre...  62.5 us
    all_to_all x3, waiting for transfers between devices, apply_pair(): lax.all_to_all(face_term(m_faces), 'rows', split_axis=0, concat_axis=0, t...  61.7 us
    another operation x18, other arithmetic, rayleigh(): inner_factor = jnp.linalg.cholesky(inner)  60.4 us
  transfers between devices with their start and end apart: 11, of which 8 were waited for; matrix products, arithmetic and copies ran while one was open for 9% of the time, Pallas kernels for 0%

profile of v1, /device:TPU:1, one launch (start us, length us, event | category | flops | bytes accessed | tf_op | source)
XLA Modules:
  0.0 1831.2 jit_solution(13353500352175629495)
XLA Ops:
  8.9 10.2 all-to-all-start.2
  26.1 9.0 convolution_multiply_fusion
  35.1 3.7 all_to_all.61
  38.8 14.5 all-to-all-start.1
  53.4 7.4 convolution_multiply_fusion.1
  64.4 48.1 %all-to-all-done.1 = f32[64,1,4608]{2,1,0:T(1,128)} async-done(((f32[64,1,4608]{2,1,0:T(1,128)}), f32[64,1,4608]{2,1,0:T(1,128)}, u32[]{:S(2)}, u32[]{:S(2)}) %all-to-all-start.1) | async-done | bytes 1179680 | tf_op jit(solution)/shard_map/all_to_all | solution.py:62
  112.5 7.3 all-to-all-start
  134.7 5.1 reduce.17
  150.4 25.8 %all-to-all-done = f32[64,1,4608]{2,1,0:T(1,128)} async-done(((f32[64,1,4608]{2,1,0:T(1,128)}), f32[64,1,4608]{2,1,0:T(1,128)}, u32[]{:S(2)}, u32[]{:S(2)}) %all-to-all-start) | async-done | bytes 1179680 | tf_op jit(solution)/shard_map/all_to_all | solution.py:61
  176.2 5.1 reduce.16
  191.3 222.1 %all-reduce.5 = (f32[1,96,1,12]{1,3,2,0:T(8,128)S(1)}, f32[1,96,1,12]{1,3,2,0:T(8,128)S(1)}) all-reduce(f32[1,96,1,12]{1,3,2,0:T(8,128)S(1)} %convolution_bitcast_fusion.19, f32[1,96,1,12]{1,3,2,0:T(8,128)S(1)} %convolution_bitcast_fusion.20), channel_id=1, replica_groups=mesh['rows'=64,'cols'=8] {'rows'}, use_global_device_ids=true, to_apply=%region_3.5 | all-reduce | flops 2304 | bytes 18432 | tf_op jit(solution)/shard_map/psum | solution.py:97
  413.4 71.6 %all_gather.36 = f32[1,96,1,96]{1,2,0,3:T(1,128)S(1)} all-gather(f32[1,96,1,12]{1,2,0,3:T(1,128)S(1)} %copy.369), channel_id=1, replica_groups=mesh['rows'=64,'cols'=8] {'cols'}, dimensions={3}, use_global_device_ids=true | all-gather | bytes 41472 | tf_op jit(solution)/shard_map/all_gather | solution.py:100
  485.4 8.8 cholesky.329
  495.5 7.4 custom-call.31
  502.9 12.8 all_gather.37
  517.1 12.8 all-gather
  533.6 4.5 all-to-all-start.3
  542.5 7.6 convolution_multiply_fusion.5
  553.2 6.2 all-to-all-start.4
  562.8 8.5 convolution_multiply_fusion.4
  575.1 14.5 all_gather.41
  592.9 13.8 all-to-all-start.5
  633.4 6.9 all-to-all-done.5
  653.4 17.2 all_gather.42
  670.6 13.4 all_gather.43
  687.1 225.0 %all-reduce.11.cloned.1.call-done = (f32[3,96,3,12]{1,3,2,0:T(8,128)}, f32[3,96,3,12]{1,3,2,0:T(8,128)}) async-done(((f32[3,96,3,12]{1,3,2,0:T(8,128)}, f32[3,96,3,12]{1,3,2,0:T(8,128)}), (f32[3,96,3,12]{1,3,2,0:T(8,128)}, f32[3,96,3,12]{1,3,2,0:T(8,128)})) %all-reduce.11.cloned.1.call-update) | async-done | bytes 82960 | tf_op jit(solution)/shard_map/psum | solution.py:97
  913.0 25.3 %all_gather.39 = f32[3,96,3,96]{1,2,0,3:T(4,128)} all-gather(f32[3,96,3,12]{1,2,0,3:T(4,128)S(1)} %copy.396), channel_id=1, replica_groups=mesh['rows'=64,'cols'=8] {'cols'}, dimensions={3}, use_global_device_ids=true | all-gather | bytes 373248 | tf_op jit(solution)/shard_map/all_gather | solution.py:99
  952.6 11.7 cholesky.342
  965.1 9.8 custom-call.46
  977.9 11.7 cholesky.361
  990.2 10.0 custom-call.47
  1010.6 5.8 while.12
  1016.9 29.5 %custom-call.52 = f32[3,128,128]{1,2,0:T(8,128)S(1)} custom-call(f32[3,128,128]{2,1,0:T(8,128)S(1)} %pad_maximum_fusion), custom_call_target="InvertDiagBlocksLowerTriangular" | custom-call | tf_op jit(solution)/shard_map/jit(_cho_solve)/triangular_solve | solution.py:115
  1047.4 14.3 all_gather.40
  1084.5 9.6 cholesky.397
  1096.0 8.2 custom-call.49
  1118.3 10.0 cholesky.408
  1130.2 8.2 custom-call.51
  1148.4 8.8 cholesky.419
  1158.5 7.4 custom-call.53
  1181.0 13.0 all-gather.1
  1197.8 4.3 all-to-all-start.6
  1206.5 7.5 convolution_multiply_fusion.3
  1217.1 9.1 all-to-all-start.7
  1227.5 8.5 convolution_multiply_fusion.2
  1239.0 20.7 %all-to-all-done.7 = f32[64,1,2304]{2,1,0:T(1,128)} async-done(((f32[64,1,2304]{2,1,0:T(1,128)}), f32[64,1,2304]{2,1,0:T(1,128)}, u32[]{:S(2)}, u32[]{:S(2)}) %all-to-all-start.7) | async-done | bytes 589856 | tf_op jit(solution)/shard_map/all_to_all | solution.py:61
  1259.7 7.5 all-to-all-start.8
  1292.2 6.7 all-to-all-done.8
  1313.5 18.6 %all_gather.47 = f32[3,96,512]{2,0,1:T(4,128)S(1)} all-gather(f32[3,12,512]{2,0,1:T(4,128)S(1)} %copy-done.27), channel_id=1, replica_groups=mesh['rows'=64,'cols'=8] {'cols'}, dimensions={1}, use_global_device_ids=true | all-gather | bytes 663552 | tf_op jit(solution)/shard_map/all_gather | solution.py:212
  1333.2 227.7 %all-reduce.9.cloned.1.call-done = (f32[3,96,3,12]{1,3,2,0:T(8,128)}, f32[3,96,3,12]{1,3,2,0:T(8,128)}) async-done(((f32[3,96,3,12]{1,3,2,0:T(8,128)}, f32[3,96,3,12]{1,3,2,0:T(8,128)}), (f32[3,96,3,12]{1,3,2,0:T(8,128)}, f32[3,96,3,12]{1,3,2,0:T(8,128)})) %all-reduce.9.cloned.1.call-update) | async-done | bytes 82960 | tf_op jit(solution)/shard_map/psum | solution.py:97
  1561.8 25.3 %all_gather.45 = f32[3,96,3,96]{1,2,0,3:T(4,128)} all-gather(f32[3,96,3,12]{1,2,0,3:T(4,128)S(1)} %copy.454), channel_id=1, replica_groups=mesh['rows'=64,'cols'=8] {'cols'}, dimensions={3}, use_global_device_ids=true | all-gather | bytes 373248 | tf_op jit(solution)/shard_map/all_gather | solution.py:99
  1601.4 11.7 cholesky.432
  1614.0 9.8 custom-call.54
  1626.7 11.7 cholesky.451
  1640.3 9.9 custom-call.55
  1660.0 5.8 while.13
  1665.9 29.5 %custom-call.60 = f32[3,128,128]{1,2,0:T(8,128)S(1)} custom-call(f32[3,128,128]{2,1,0:T(8,128)S(1)} %pad_maximum_fusion.1), custom_call_target="InvertDiagBlocksLowerTriangular" | custom-call | tf_op jit(solution)/shard_map/jit(_cho_solve)/triangular_solve | solution.py:115
  1696.4 14.3 all_gather.46
  1733.5 9.6 cholesky.487
  1745.0 8.2 custom-call.57
  1767.3 9.8 cholesky.498
  1779.0 8.2 custom-call.59
  1797.2 8.8 cholesky.509
  1807.3 7.4 custom-call.61
  (524 shorter events, 369.8 us)
Async XLA Ops:
  7.2 46.2 %copy-start = (bf16[1,64,3,64,64]{4,3,2,1,0:T(8,128)(2,1)S(1)}, bf16[1,64,3,64,64]{4,3,2,1,0:T(8,128)(2,1)}, u32[]{:S(2)}) copy-start(bf16[1,64,3,64,64]{4,3,2,1,0:T(8,128)(2,1)} %param.26) | copy-start | bytes 4718596
  8.9 29.9 %all-to-all-start.2 = ((f32[8,1,12,512]{3,1,2,0:T(1,128)}), f32[8,1,12,512]{3,1,2,0:T(1,128)S(1)}, u32[]{:S(2)}, u32[]{:S(2)}) async-start(f32[8,1,12,512]{3,1,2,0:T(1,128)} %stack.82), calls=%async_computation.2 | async-start | bytes 393216 | tf_op jit(solution)/shard_map/all_to_all | solution.py:84
  19.9 164.7 %copy-start.52 = (s32[192]{0:T(256)}, s32[192]{0:T(256)S(1)}, u32[]{:S(2)}) copy-start(s32[192]{0:T(256)S(1)} %eq.37) | copy-start | bytes 2308
  22.8 3.0 copy-start.62
  26.1 27.3 %copy-start.59 = (f32[192]{0:T(256)}, f32[192]{0:T(256)S(1)}, u32[]{:S(2)}) copy-start(f32[192]{0:T(256)S(1)} %convert_element_type.19) | copy-start | bytes 2308
  38.8 22.0 %copy-start.17 = (f32[8,1,12,512]{3,1,2,0:T(1,128)}, f32[8,1,12,512]{3,1,2,0:T(1,128)S(1)}, u32[]{:S(2)}) copy-start(f32[8,1,12,512]{3,1,2,0:T(1,128)S(1)} %all-to-all-done.2) | copy-start | bytes 589828
  38.8 73.7 %all-to-all-start.1 = ((f32[64,1,4608]{2,1,0:T(1,128)}), f32[64,1,4608]{2,1,0:T(1,128)}, u32[]{:S(2)}, u32[]{:S(2)}) async-start(f32[64,1,4608]{2,1,0:T(1,128)} %all_to_all.61), calls=%async_computation.1 | async-start | bytes 2359296 | tf_op jit(solution)/shard_map/all_to_all | solution.py:62
  64.4 56.1 %copy-start.63 = (s32[8]{0:T(128)S(1)}, s32[8]{0:T(128)}, u32[]{:S(2)}) copy-start(s32[8]{0:T(128)} %param.25) | copy-start | bytes 100
  64.4 56.2 %copy-start.11 = (bf16[8,64,64]{2,1,0:T(8,128)(2,1)S(1)}, bf16[8,64,64]{2,1,0:T(8,128)(2,1)}, u32[]{:S(2)}) copy-start(bf16[8,64,64]{2,1,0:T(8,128)(2,1)} %param.20) | copy-start | bytes 196612
  112.5 63.7 %all-to-all-start = ((f32[64,1,4608]{2,1,0:T(1,128)}), f32[64,1,4608]{2,1,0:T(1,128)}, u32[]{:S(2)}, u32[]{:S(2)}) async-start(f32[64,1,4608]{2,1,0:T(1,128)} %all_to_all.60), calls=%async_computation | async-start | bytes 2359296 | tf_op jit(solution)/shard_map/all_to_all | solution.py:61
  120.6 10.0 copy-start.57
  120.7 6.5 copy-start.45
  120.7 5.4 copy-start.48
  124.6 5.0 copy-start.13
  126.1 4.5 copy-start.32
  142.7 2.8 copy-start.6
  142.7 2.8 copy-start.29
  142.7 2.8 copy-start.31
  184.7 2.8 copy-start.3
  184.7 2.8 copy-start.28
  184.7 2.8 copy-start.30
  188.1 328.9 %copy-start.34 = (f32[1,12,512]{2,1,0:T(8,128)S(1)}, f32[1,12,512]{2,1,0:T(8,128)}, u32[]{:S(2)}) copy-start(f32[1,12,512]{2,1,0:T(8,128)} %reshape.282) | copy-start | bytes 73732
  190.0 341.8 %copy-start.33 = (f32[12,512]{1,0:T(8,128)S(1)}, f32[12,512]{1,0:T(8,128)}, u32[]{:S(2)}) copy-start(f32[12,512]{1,0:T(8,128)} %param.18) | copy-start | bytes 73732
  530.6 7.5 copy-start.53
  533.6 19.6 %all-to-all-start.3 = ((f32[8,3,12,512]{3,2,1,0:T(8,128)}), f32[8,3,12,512]{3,2,1,0:T(8,128)}, u32[]{:S(2)}, u32[]{:S(2)}) async-start(f32[8,3,12,512]{3,2,1,0:T(8,128)} %stack.86), calls=%async_computation.3 | async-start | bytes 1572864 | tf_op jit(solution)/shard_map/all_to_all | solution.py:84
  538.1 4.4 copy-start.60
  550.1 11.9 copy-start.43
  553.2 39.8 %all-to-all-start.4 = ((f32[64,1,2304]{2,1,0:T(1,128)}), f32[64,1,2304]{2,1,0:T(1,128)}, u32[]{:S(2)}, u32[]{:S(2)}) async-start(f32[64,1,2304]{2,1,0:T(1,128)} %all_to_all.62), calls=%async_computation.4 | async-start | bytes 1179648 | tf_op jit(solution)/shard_map/all_to_all | solution.py:61
  571.3 3.0 copy-start.42
  574.4 16.2 copy-start.46
  575.1 15.5 copy-start.4
  589.6 18.0 copy-start.51
  589.6 18.6 %copy-start.49 = (s32[8,4]{0,1:T(4,128)S(1)}, s32[8,4]{0,1:T(4,128)}, u32[]{:S(2)}) copy-start(s32[8,4]{0,1:T(4,128)} %param.24) | copy-start | bytes 388
  591.6 21.8 %copy-start.12 = (bf16[8,64,64]{2,1,0:T(8,128)(2,1)S(1)}, bf16[8,64,64]{2,1,0:T(8,128)(2,1)}, u32[]{:S(2)}) copy-start(bf16[8,64,64]{2,1,0:T(8,128)(2,1)} %param.20) | copy-start | bytes 196612
  592.9 47.4 %all-to-all-start.5 = ((f32[64,1,2304]{2,1,0:T(1,128)}), f32[64,1,2304]{2,1,0:T(1,128)}, u32[]{:S(2)}, u32[]{:S(2)}) async-start(f32[64,1,2304]{2,1,0:T(1,128)} %all_to_all.63), calls=%async_computation.5 | async-start | bytes 1179648 | tf_op jit(solution)/shard_map/all_to_all | solution.py:62
  606.7 305.4 %all-reduce.11.cloned.1.call-start = ((), (), s32[]{:S(2)}) async-start(), calls=%async_computation.10 | async-start | bytes 294912 | tf_op jit(solution)/shard_map/psum | solution.py:97
  623.6 4.9 copy-start.39
  623.6 4.9 copy-start.41
  626.3 3.9 copy-start.22
  633.4 12.7 copy-start.54
  646.2 4.0 copy-start.21
  952.6 57.2 %copy-start.66 = (s32[2]{0:T(128)S(1)}, s32[2]{0:T(128)}, u32[]{:S(2)}) copy-start(s32[2]{0:T(128)} %iota_multiply_fusion) | copy-start | bytes 28
  965.1 51.2 %copy-start.19 = (f32[128,96]{1,0:T(8,128)S(1)}, f32[128,96]{1,0:T(8,128)}, u32[]{:S(2)}) copy-start(f32[128,96]{1,0:T(8,128)} %pad_convert_fusion) | copy-start | bytes 147460
  1145.9 12.7 copy-start.18
  1194.7 7.3 copy-start.55
  1197.8 19.3 %all-to-all-start.6 = ((f32[8,3,12,512]{3,2,1,0:T(8,128)}), f32[8,3,12,512]{3,2,1,0:T(8,128)}, u32[]{:S(2)}, u32[]{:S(2)}) async-start(f32[8,3,12,512]{3,2,1,0:T(8,128)} %stack.95), calls=%async_computation.6 | async-start | bytes 1572864 | tf_op jit(solution)/shard_map/all_to_all | solution.py:84
  1202.0 4.5 copy-start.61
  1217.1 42.7 %all-to-all-start.7 = ((f32[64,1,2304]{2,1,0:T(1,128)}), f32[64,1,2304]{2,1,0:T(1,128)}, u32[]{:S(2)}, u32[]{:S(2)}) async-start(f32[64,1,2304]{2,1,0:T(1,128)} %all_to_all.64), calls=%async_computation.7 | async-start | bytes 1179648 | tf_op jit(solution)/shard_map/all_to_all | solution.py:61
  1236.0 31.5 %copy-start.47 = (f32[8,4]{1,0:T(8,128)S(1)}, f32[8,4]{1,0:T(8,128)}, u32[]{:S(2)}) copy-start(f32[8,4]{1,0:T(8,128)} %copy-done.45) | copy-start | bytes 388
  1236.0 33.0 %copy-start.50 = (s32[8,4]{0,1:T(4,128)S(1)}, s32[8,4]{0,1:T(4,128)}, u32[]{:S(2)}) copy-start(s32[8,4]{0,1:T(4,128)} %param.24) | copy-start | bytes 388
  1239.0 33.2 %copy-start.58 = (f32[8,4]{0,1:T(4,128)S(1)}, f32[8,4]{0,1:T(4,128)}, u32[]{:S(2)}) copy-start(f32[8,4]{0,1:T(4,128)} %copy-done.57) | copy-start | bytes 388
  1259.7 39.1 %all-to-all-start.8 = ((f32[64,1,2304]{2,1,0:T(1,128)}), f32[64,1,2304]{2,1,0:T(1,128)}, u32[]{:S(2)}, u32[]{:S(2)}) async-start(f32[64,1,2304]{2,1,0:T(1,128)} %all_to_all.65), calls=%async_computation.8 | async-start | bytes 1179648 | tf_op jit(solution)/shard_map/all_to_all | solution.py:62
  1267.2 293.7 %all-reduce.9.cloned.1.call-start = ((), (), s32[]{:S(2)}) async-start(), calls=%async_computation.9 | async-start | bytes 294912 | tf_op jit(solution)/shard_map/psum | solution.py:97
  1267.5 7.7 copy-start.14
  1267.5 8.6 copy-start.9
  1267.5 9.6 copy-start.10
  1282.3 5.9 copy-start.56
  1285.6 4.8 copy-start.38
  1285.6 4.8 copy-start.40
  1304.7 4.0 copy-start.37
  1304.7 6.4 copy-start.35
  1306.9 6.6 copy-start.27
  1601.4 58.6 %copy-start.65 = (s32[2,2]{1,0:T(2,128)S(1)}, s32[2,2]{1,0:T(2,128)}, u32[]{:S(2)}) copy-start(s32[2,2]{1,0:T(2,128)} %copy-done.64) | copy-start | bytes 52
  1614.0 51.8 %copy-start.20 = (f32[128,96]{1,0:T(8,128)S(1)}, f32[128,96]{1,0:T(8,128)}, u32[]{:S(2)}) copy-start(f32[128,96]{1,0:T(8,128)} %pad_convert_fusion) | copy-start | bytes 147460
  (14 other events, 11.5 us)
Sparse Core Ops, SparseCore 0:
  670.7 241.4 all-reduce.10
  1313.6 247.2 all-reduce.8
